TPU v7x, 32 devices: a whole 2x2x4 slice. The times are simulated.
32 devices in a mesh: dp: 16 (over z, y, x), ctx: 2 (over core).
Axes of the slice: x: 2, y: 2, z: 4, core: 2. Of those that a mesh axis runs over, the one named last changes fastest.
Arguments:
- inputs: bfloat16 [16, 4, 16, 16, 128], P('dp', 'ctx'), may hold values from -90 to 90
- cotangent: bfloat16 [16, 4, 16, 16, 128], P('dp', 'ctx'), may hold values from -18 to 18
- conv_weight: bfloat16 [3, 3, 3, 128, 128], replicated, may hold values from -0.109375 to 0.109375
- norm_gain: float32 [128], replicated, may hold values from 0.1 to 1.9
- norm_bias: float32 [128], replicated, may hold values from -3 to 3
Outputs:
- input_grad: bfloat16 [16, 4, 16, 16, 128], P('dp', 'ctx')
- weight_grad: float32 [3, 3, 3, 128, 128], replicated
- gain_grad: float32 [128], replicated
- bias_grad: float32 [128], replicated
All inputs are finite; a program needn't handle non-finite values.
Results may differ from a plain program's by a relative error of at most 0.0027.
Values may be sent and summed in bfloat16 or wider, within the bound.
A program may use at most 64 MiB of HBM per device.

v0:
```python
import jax
import jax.numpy as jnp
from jax import lax
from jax.sharding import PartitionSpec as P

GROUPS = 32
epsilon = 1e-06


def from_behind(x, axis, by):
    count = lax.axis_size(axis)
    pairs = [(i, i + by) for i in range(count) if 0 <= i + by < count]
    return lax.ppermute(x, axis, pairs)


def group_average(per_channel, members):
    grouped = per_channel.reshape(GROUPS, -1).sum(axis=1, keepdims=True) / members
    return jnp.broadcast_to(grouped, (GROUPS, per_channel.shape[0] // GROUPS)).reshape(-1)


def kernel_terms(padded_act, grad_flat, frames_n, side_len, channels):
    pieces = []
    for tap_time in range(3):
        for tap_row in range(3):
            columns = jnp.concatenate(
                [
                    padded_act[
                        tap_time : tap_time + frames_n,
                        tap_row : tap_row + side_len,
                        tap_col : tap_col + side_len,
                    ]
                    for tap_col in range(3)
                ],
                axis=-1,
            ).reshape(-1, 3 * channels)
            pieces.append(
                lax.dot_general(
                    columns, grad_flat, (((0,), (0,)), ((), ())), preferred_element_type=jnp.float32
                )
            )
    return jnp.stack(pieces).reshape(3, 3, 3, channels, channels)


def spread_back(grad_ext, weight_turned, frames_out, side_len, channels):
    total_grad = jnp.zeros((frames_out * side_len * side_len, channels), jnp.float32)
    for tap_time in range(3):
        for tap_row in range(3):
            columns = jnp.concatenate(
                [
                    grad_ext[
                        2 - tap_time : 2 - tap_time + frames_out,
                        2 - tap_row : 2 - tap_row + side_len,
                        2 - tap_col : 2 - tap_col + side_len,
                    ]
                    for tap_col in range(3)
                ],
                axis=-1,
            ).reshape(-1, 3 * channels)
            total_grad = total_grad + jnp.dot(
                columns,
                weight_turned[tap_time, tap_row].reshape(3 * channels, channels),
                preferred_element_type=jnp.float32,
            )
    return total_grad.reshape(frames_out, side_len, side_len, channels)


def plane_back(plane, weight_plane, side_len, channels):
    padded = jnp.pad(plane, ((1, 1), (1, 1), (0, 0)))
    total_grad = jnp.zeros((side_len * side_len, channels), jnp.float32)
    for tap_row in range(3):
        columns = jnp.concatenate(
            [
                padded[2 - tap_row : 2 - tap_row + side_len, 2 - tap_col : 2 - tap_col + side_len]
                for tap_col in range(3)
            ],
            axis=-1,
        ).reshape(-1, 3 * channels)
        total_grad = total_grad + jnp.dot(
            columns,
            weight_plane[tap_row].reshape(3 * channels, channels),
            preferred_element_type=jnp.float32,
        )
    return total_grad.reshape(side_len, side_len, channels)


def body(inputs, cotangent, conv_weight, norm_gain, norm_bias):
    frames_n, side_len, channels = (inputs.shape[1], inputs.shape[2], inputs.shape[4])
    ctx_count = lax.axis_size("ctx")
    leading = lax.axis_index("ctx") == 0
    members = frames_n * side_len * side_len * ctx_count * (channels // GROUPS)
    values = inputs[0].astype(jnp.float32)
    flat_values = values.reshape(-1, channels)
    totals, squares = lax.psum(
        (flat_values.sum(axis=0), (flat_values * flat_values).sum(axis=0)), "ctx"
    )
    average = group_average(totals, members)
    spread = group_average(squares, members) - average * average
    inverse_std = lax.rsqrt(spread + epsilon)
    normed_val = (values - average) * inverse_std
    shifted_val = normed_val * norm_gain + norm_bias
    activation = jax.nn.silu(shifted_val).astype(jnp.bfloat16)
    prior = from_behind(activation, "ctx", 1)
    prior = jnp.where(leading, jnp.broadcast_to(activation[:1], prior.shape), prior)
    padded_act = jnp.concatenate([prior, activation], axis=0)
    padded_act = jnp.pad(padded_act, ((0, 0), (1, 1), (1, 1), (0, 0)))
    grad_local = cotangent[0]
    after_frames = from_behind(grad_local, "ctx", -1)
    kernel_sum = kernel_terms(
        padded_act, grad_local.reshape(-1, channels), frames_n, side_len, channels
    )
    grad_ext = jnp.concatenate([grad_local, after_frames], axis=0)
    grad_ext = jnp.pad(grad_ext, ((0, 0), (1, 1), (1, 1), (0, 0)))
    weight_turned = jnp.transpose(conv_weight, (0, 1, 2, 4, 3))
    pad_grad = spread_back(grad_ext, weight_turned, frames_n, side_len, channels)

    def fold_terms():
        first_part = plane_back(grad_local[0], weight_turned[0], side_len, channels)
        second_part = plane_back(grad_local[1], weight_turned[0], side_len, channels)
        third_part = plane_back(grad_local[0], weight_turned[1], side_len, channels)
        return first_part + (second_part + third_part)

    def fold_empty():
        return jnp.zeros((side_len, side_len, channels), jnp.float32)

    folded = lax.cond(leading, fold_terms, fold_empty)
    act_grad = pad_grad.at[0].add(folded)
    sigmoid_val = jax.nn.sigmoid(shifted_val)
    pre_grad = act_grad * sigmoid_val * (1.0 + shifted_val * (1.0 - sigmoid_val))
    normed_grad = pre_grad * norm_gain
    first_total, second_total = lax.psum(
        (
            normed_grad.reshape(-1, channels).sum(axis=0),
            (normed_grad * normed_val).reshape(-1, channels).sum(axis=0),
        ),
        "ctx",
    )
    first_mean = group_average(first_total, members)
    second_mean = group_average(second_total, members)
    input_grad = (inverse_std * (normed_grad - first_mean - normed_val * second_mean)).astype(
        jnp.bfloat16
    )[None]
    gain_part = (pre_grad * normed_val).reshape(-1, channels).sum(axis=0)
    bias_part = pre_grad.reshape(-1, channels).sum(axis=0)
    kernel_all, gain_all, bias_all = lax.psum((kernel_sum, gain_part, bias_part), ("dp", "ctx"))
    cell_total = lax.axis_size("dp") * ctx_count * frames_n * side_len * side_len
    scale_val = 1.0 / jnp.sqrt(jnp.float32(cell_total))
    return (input_grad, kernel_all * scale_val, gain_all * scale_val, bias_all * scale_val)


def solution(mesh):
    placed = (P("dp", "ctx", None, None, None), P("dp", "ctx", None, None, None), P(), P(), P())
    return jax.shard_map(
        body,
        mesh=mesh,
        in_specs=placed,
        out_specs=(P("dp", "ctx", None, None, None), P(), P(), P()),
        check_vma=False,
    )
```

profile of v0, /device:TPU:0, one launch (start us, length us, event | category | flops | bytes accessed | tf_op | source)
XLA Modules:
  0.0 180.4 jit_solution(15650351091484848257)
XLA Ops:
  7.2 1.3 collective-permute-start
  8.5 2.0 %copy.10 = bf16[3,3,3,128,128]{3,4,2,1,0:T(8,128)(2,1)S(1)} copy(bf16[3,3,3,128,128]{4,3,2,1,0:T(8,128)(2,1)} %param.11) | data formatting | bytes 1769472 | tf_op args[2]
  11.0 4.4 %all-reduce.6 = (f32[32,4]{1,0:T(8,128)S(1)}, f32[32,4]{1,0:T(8,128)S(1)}) all-reduce(f32[32,4]{1,0:T(8,128)S(1)} %reshape.233, f32[32,4]{1,0:T(8,128)S(1)} %reshape.231), channel_id=1, replica_groups=mesh['dp'=16,'ctx'=2] {'ctx'}, use_global_device_ids=true, to_apply=%region_4.0 | all-reduce | flops 256 | bytes 2048 | tf_op jit(solution)/shard_map/psum | solution.py:93
  16.0 2.3 %conditional.1 = (f32[1,16,16,128]{3,2,1,0:T(8,128)S(1)}) conditional(s32[]{:T(128)} %convert_element_type.28, () %tuple.20, (bf16[2,16,16,128]{3,2,1,0:T(8,128)(2,1)S(1)}, bf16[3,3,3,128,128]{4,3,2,1,0:T(8,128)(2,1)S(1)}) %tuple.120), branch_computations={%region_6.7_spmd, %region_7.8_spmd} | conditional | flops 230883328 | bytes 9207816 | solution.py:125
  16.1 0.2 pad_slice_fusion.2
  16.3 0.2 fusion.55
  16.5 0.2 convolution_add_fusion.3
  16.7 0.2 convolution_add_fusion.2
  17.0 0.2 fusion.56
  17.2 0.2 fusion.54
  17.4 0.2 convolution_add_fusion.5
  17.6 0.2 convolution_add_fusion.1
  17.8 0.2 convolution_add_fusion.4
  18.0 0.2 fusion.1
  18.3 0.1 pad_slice_fusion.41
  18.5 0.4 pad_slice_fusion.42
  19.0 0.3 fusion.57
  19.3 0.3 convolution_add_fusion.13
  19.5 0.1 pad_maximum_fusion.9
  19.7 0.3 convolution_add_fusion.12
  19.9 0.3 convolution_add_fusion.11
  20.3 0.3 convolution_add_fusion.10
  20.6 0.3 convolution_add_fusion.9
  21.0 0.3 convolution_add_fusion.8
  21.3 0.3 convolution_add_fusion.7
  21.6 0.3 convolution_add_fusion.6
  21.9 0.2 fusion.45
  22.3 3.4 %all-reduce.5 = (f32[32,4]{1,0:T(8,128)S(1)}, f32[32,4]{1,0:T(8,128)S(1)}) all-reduce(f32[32,4]{1,0:T(8,128)S(1)} %reshape.246, f32[32,4]{1,0:T(8,128)S(1)} %reshape.245), channel_id=1, replica_groups=mesh['dp'=16,'ctx'=2] {'ctx'}, use_global_device_ids=true, to_apply=%region_12.13 | all-reduce | flops 256 | bytes 2048 | tf_op jit(solution)/shard_map/psum | solution.py:130
  26.2 2.3 %collective-permute-start.1 = (bf16[2,16,16,128]{3,2,1,0:T(8,128)(2,1)S(1)}, bf16[2,16,16,128]{3,2,1,0:T(8,128)(2,1)S(1)}, u32[]{:S(2)}, u32[]{:S(2)}) collective-permute-start(bf16[2,16,16,128]{3,2,1,0:T(8,128)(2,1)S(1)} %get-tuple-element.130), channel_id=1, source_target_pairs={{0,1},{2,3},{4,5},{6,7},{8,9},{10,11},{12,13},{14,15},{16,17},{18,... | collective-permute-start | bytes 393224 | tf_op jit(solution)/shard_map/ppermute | solution.py:13
  28.4 0.9 collective-permute-done.1
  29.5 0.1 pad_slice_fusion.17
  29.6 0.4 pad_slice_fusion.18
  30.1 0.3 fusion.18
  30.5 0.3 fusion.17
  30.9 0.3 fusion.16
  31.3 0.3 fusion.15
  31.7 0.3 fusion.14
  32.0 0.3 fusion.13
  32.4 0.3 fusion.12
  32.8 0.3 fusion.11
  33.1 0.3 fusion.10
  33.5 1.2 copy-done.1
  34.9 42.1 %all-reduce.4 = (f32[128]{0:T(128)S(1)}, f32[128]{0:T(128)S(1)}) all-reduce(f32[128]{0:T(128)S(1)} %get-tuple-element.26, f32[128]{0:T(128)S(1)} %get-tuple-element.29), channel_id=1, replica_groups=mesh['dp'=16,'ctx'=2] {'dp','ctx'}, use_global_device_ids=true, to_apply=%region_16.17 | all-reduce | flops 256 | bytes 2048 | tf_op jit(solution)/shard_map/psum | solution.py:144
  77.0 0.5 broadcast_multiply_fusion.2
  77.5 0.5 broadcast_multiply_fusion.1
  78.0 0.7 fusion.46
  78.8 91.9 %all-reduce.9.cloned.1.call-done = f32[3,3,3,128,128]{4,3,2,1,0:T(8,128)} async-done(((f32[3,3,3,128,128]{4,3,2,1,0:T(8,128)}), f32[3,3,3,128,128]{4,3,2,1,0:T(8,128)}) %all-reduce.9.cloned.1.call-update) | async-done | bytes 1769488 | tf_op jit(solution)/shard_map/psum | solution.py:144
  170.7 2.9 %broadcast_multiply_fusion = f32[3,3,3,128,128]{4,3,2,1,0:T(8,128)} fusion(f32[3,3,3,128,128]{4,3,2,1,0:T(8,128)} %all-reduce.9.cloned.1.call-done), kind=kLoop, calls=%fused_computation.113 | loop fusion | flops 442368 | bytes 3538944 | tf_op jit(solution)/shard_map/mul | solution.py:147
  (61 shorter events, 3.0 us)
Async XLA Ops:
  7.2 163.5 %all-reduce.9.cloned.1.call-start = ((), (), s32[]{:S(2)}) async-start(), calls=%async_computation | async-start | bytes 3538944 | tf_op jit(solution)/shard_map/psum | solution.py:144
  7.2 11.1 %collective-permute-start = (bf16[2,16,16,128]{3,2,1,0:T(8,128)(2,1)}, bf16[2,16,16,128]{3,2,1,0:T(8,128)(2,1)S(1)}, u32[]{:S(2)}, u32[]{:S(2)}) collective-permute-start(bf16[2,16,16,128]{3,2,1,0:T(8,128)(2,1)} %bitcast.196), channel_id=1, source_target_pairs={{1,0},{3,2},{5,4},{7,6},{9,8},{11,10},{13,12},{15,14},{17,16},{19,... | collective-permute-start | bytes 393224 | tf_op jit(solution)/shard_map/ppermute | solution.py:13
  8.5 2.2 %copy-start.2 = (bf16[1,2,16,16,128]{4,3,2,1,0:T(8,128)(2,1)S(1)}, bf16[1,2,16,16,128]{4,3,2,1,0:T(8,128)(2,1)}, u32[]{:S(2)}) copy-start(bf16[1,2,16,16,128]{4,3,2,1,0:T(8,128)(2,1)} %param.9) | copy-start | bytes 393220
  8.5 7.3 %copy-start = (bf16[1,2,16,16,128]{4,3,2,1,0:T(8,128)(2,1)S(1)}, bf16[1,2,16,16,128]{4,3,2,1,0:T(8,128)(2,1)}, u32[]{:S(2)}) copy-start(bf16[1,2,16,16,128]{4,3,2,1,0:T(8,128)(2,1)} %param.10) | copy-start | bytes 393220
  21.0 0.9 copy-start.3
  21.0 0.9 copy-start.4
  26.2 3.2 %collective-permute-start.1 = (bf16[2,16,16,128]{3,2,1,0:T(8,128)(2,1)S(1)}, bf16[2,16,16,128]{3,2,1,0:T(8,128)(2,1)S(1)}, u32[]{:S(2)}, u32[]{:S(2)}) collective-permute-start(bf16[2,16,16,128]{3,2,1,0:T(8,128)(2,1)S(1)} %get-tuple-element.130), channel_id=1, source_target_pairs={{0,1},{2,3},{4,5},{6,7},{8,9},{10,11},{12,13},{14,15},{16,17},{18,... | collective-permute-start | bytes 393224 | tf_op jit(solution)/shard_map/ppermute | solution.py:13
  33.5 1.2 copy-start.1
Sparse Core Ops, SparseCore 0:
  34.8 135.8 all-reduce.8
where the time goes:
time: 181 us; the launch traced here: 180 us
  waiting for transfers between devices  92.9 us (51%)
  blocking collectives  49.9 us (28%)
  between operations  14.6 us (8%)
  matrix products  6.96 us (4%)
  other arithmetic  6.58 us (4%)
  local copies, waits for them, and re-layouts  5.8 us (3%)
  starting transfers between devices  3.58 us (2%)
    psum x1, waiting for transfers between devices, body(): lax.psum((kernel_sum, gain_part, bias_part), ('dp', 'ctx'))  91.9 us
    psum x1, blocking collectives, body(): lax.psum((kernel_sum, gain_part, bias_part), ('dp', 'ctx'))  42.1 us
    psum x1, blocking collectives, body(): lax.psum((flat_values.sum(axis=0), (flat_values * flat_values).sum(axis=0...  4.37 us
  transfers between devices with their start and end apart: 3, of which 2 were waited for; matrix products, arithmetic and copies ran while one was open for 4% of the time, Pallas kernels for 0%

commit v1 on v0

--- a/solution.py
+++ b/solution.py
@@ -141,7 +141,9 @@
     )[None]
     gain_part = (pre_grad * normed_val).reshape(-1, channels).sum(axis=0)
     bias_part = pre_grad.reshape(-1, channels).sum(axis=0)
-    kernel_all, gain_all, bias_all = lax.psum((kernel_sum, gain_part, bias_part), ("dp", "ctx"))
+    kernel_all, gain_all, bias_all = lax.psum(
+        lax.psum((kernel_sum, gain_part, bias_part), "ctx"), "dp"
+    )
     cell_total = lax.axis_size("dp") * ctx_count * frames_n * side_len * side_len
     scale_val = 1.0 / jnp.sqrt(jnp.float32(cell_total))
     return (input_grad, kernel_all * scale_val, gain_all * scale_val, bias_all * scale_val)

time: 181 us -> 192 us (1.061)
  waiting for transfers between devices: 92.9 us -> 104 us
    psum x1 -> x2, waiting for transfers between devices: 91.9 us -> 103 us  [the longest x1 79.7 us: body(): lax.psum(lax.psum((kernel_sum, gain_part, bias_part), 'ctx'), 'dp')]
  transfers between devices with their start and end apart: 3 -> 4, of which waited for: 2 -> 3; matrix products, arithmetic and copies ran while one was open for 4% -> 4% of each run, Pallas kernels for 0% -> 0%
where the time goes in v1:
time: 192 us; the launch traced here: 191 us
  waiting for transfers between devices  104 us (54%)
  blocking collectives  50.4 us (26%)
  between operations  14.6 us (8%)
  matrix products  6.96 us (4%)
  other arithmetic  6.57 us (3%)
  local copies, waits for them, and re-layouts  5.8 us (3%)
  starting transfers between devices  2.67 us (1%)
    psum x1, waiting for transfers between devices, body(): lax.psum(lax.psum((kernel_sum, gain_part, bias_part), 'ctx'), 'dp')  79.7 us
    psum x1, blocking collectives, body(): lax.psum(lax.psum((kernel_sum, gain_part, bias_part), 'ctx'), 'dp')  42.6 us
    psum x1, waiting for transfers between devices, body(): lax.psum((kernel_sum, gain_part, bias_part), 'ctx')  23.5 us
    psum x1, blocking collectives, body(): lax.psum((flat_values.sum(axis=0), (flat_values * flat_values).sum(axis=0...  4.37 us
  transfers between devices with their start and end apart: 4, of which 3 were waited for; matrix products, arithmetic and copies ran while one was open for 4% of the time, Pallas kernels for 0%

profile of v1, /device:TPU:0, one launch (start us, length us, event | category | flops | bytes accessed | tf_op | source)
XLA Modules:
  0.0 191.4 jit_solution(1906986505425886137)
XLA Ops:
  7.2 1.3 collective-permute-start
  8.5 2.0 %copy.10 = bf16[3,3,3,128,128]{3,4,2,1,0:T(8,128)(2,1)S(1)} copy(bf16[3,3,3,128,128]{4,3,2,1,0:T(8,128)(2,1)} %param.11) | data formatting | bytes 1769472 | tf_op args[2]
  11.0 4.4 %all-reduce.6 = (f32[32,4]{1,0:T(8,128)S(1)}, f32[32,4]{1,0:T(8,128)S(1)}) all-reduce(f32[32,4]{1,0:T(8,128)S(1)} %reshape.233, f32[32,4]{1,0:T(8,128)S(1)} %reshape.231), channel_id=1, replica_groups=mesh['dp'=16,'ctx'=2] {'ctx'}, use_global_device_ids=true, to_apply=%region_4.0 | all-reduce | flops 256 | bytes 2048 | tf_op jit(solution)/shard_map/psum | solution.py:93
  16.0 2.3 %conditional.1 = (f32[1,16,16,128]{3,2,1,0:T(8,128)S(1)}) conditional(s32[]{:T(128)} %convert_element_type.28, () %tuple.20, (bf16[2,16,16,128]{3,2,1,0:T(8,128)(2,1)S(1)}, bf16[3,3,3,128,128]{4,3,2,1,0:T(8,128)(2,1)S(1)}) %tuple.122), branch_computations={%region_6.7_spmd, %region_7.8_spmd} | conditional | flops 230883328 | bytes 9207816 | solution.py:125
  16.1 0.2 pad_slice_fusion.2
  16.3 0.2 fusion.55
  16.5 0.2 convolution_add_fusion.3
  16.7 0.2 convolution_add_fusion.2
  17.0 0.2 fusion.56
  17.2 0.2 fusion.54
  17.4 0.2 convolution_add_fusion.5
  17.6 0.2 convolution_add_fusion.1
  17.8 0.2 convolution_add_fusion.4
  18.0 0.2 fusion.1
  18.3 0.1 pad_slice_fusion.41
  18.5 0.4 pad_slice_fusion.42
  19.0 0.3 fusion.57
  19.3 0.3 convolution_add_fusion.13
  19.6 0.3 convolution_add_fusion.12
  19.9 0.3 convolution_add_fusion.11
  20.3 0.3 convolution_add_fusion.10
  20.6 0.3 convolution_add_fusion.9
  21.0 0.3 convolution_add_fusion.8
  21.3 0.3 convolution_add_fusion.7
  21.5 0.3 convolution_add_fusion.6
  21.9 0.2 fusion.45
  22.1 1.3 collective-permute-start.1
  23.4 0.9 collective-permute-done.1
  24.4 0.1 pad_slice_fusion.17
  24.6 0.4 pad_slice_fusion.18
  25.1 0.3 fusion.18
  25.5 0.3 fusion.17
  25.9 0.3 fusion.16
  26.3 0.3 fusion.15
  26.6 0.3 fusion.14
  27.0 0.3 fusion.13
  27.4 0.3 fusion.12
  27.7 0.3 fusion.11
  28.1 0.3 fusion.10
  28.5 1.2 copy-done.1
  29.7 23.5 %all-reduce.10.cloned.1.call-done = f32[3,3,3,128,128]{4,3,2,1,0:T(8,128)} async-done(((f32[3,3,3,128,128]{4,3,2,1,0:T(8,128)}), f32[3,3,3,128,128]{4,3,2,1,0:T(8,128)}) %all-reduce.10.cloned.1.call-update) | async-done | bytes 1769488 | tf_op jit(solution)/shard_map/psum | solution.py:145
  53.5 3.5 %all-reduce.5 = (f32[32,4]{1,0:T(8,128)S(1)}, f32[32,4]{1,0:T(8,128)S(1)}, f32[128]{0:T(128)S(1)}, f32[128]{0:T(128)S(1)}) all-reduce(f32[32,4]{1,0:T(8,128)S(1)} %reshape.246, f32[32,4]{1,0:T(8,128)S(1)} %reshape.245, f32[128]{0:T(128)S(1)} %get-tuple-element.26, ...), channel_id=1, replica_groups=mesh['dp'=16,'ctx'=2] {'ctx'}, use_global_device_ids=true, to_apply=%region_12.13 | all-reduce | flops 512 | bytes 4096 | tf_op jit(solution)/shard_map/psum | solution.py:130
  57.6 42.6 %all-reduce.4 = (f32[128]{0:T(128)S(1)}, f32[128]{0:T(128)S(1)}) all-reduce(f32[128]{0:T(128)S(1)} %get-tuple-element.36, f32[128]{0:T(128)S(1)} %get-tuple-element.37), channel_id=1, replica_groups=mesh['dp'=16,'ctx'=2] {'dp'}, use_global_device_ids=true, to_apply=%region_18.19 | all-reduce | flops 256 | bytes 2048 | tf_op jit(solution)/shard_map/psum | solution.py:144
  100.2 0.5 broadcast_multiply_fusion.2
  100.7 0.5 broadcast_multiply_fusion.1
  101.2 0.7 fusion.46
  102.0 79.7 %all-reduce.12.cloned.1.call-done = f32[3,3,3,128,128]{4,3,2,1,0:T(8,128)} async-done(((f32[3,3,3,128,128]{4,3,2,1,0:T(8,128)}), f32[3,3,3,128,128]{4,3,2,1,0:T(8,128)}) %all-reduce.12.cloned.1.call-update) | async-done | bytes 1769488 | tf_op jit(solution)/shard_map/psum | solution.py:144
  181.7 2.9 %broadcast_multiply_fusion = f32[3,3,3,128,128]{4,3,2,1,0:T(8,128)} fusion(f32[3,3,3,128,128]{4,3,2,1,0:T(8,128)} %all-reduce.12.cloned.1.call-done), kind=kLoop, calls=%fused_computation.113 | loop fusion | flops 442368 | bytes 3538944 | tf_op jit(solution)/shard_map/mul | solution.py:149
  (64 shorter events, 3.1 us)
Async XLA Ops:
  7.2 46.1 %all-reduce.10.cloned.1.call-start = ((), (), s32[]{:S(2)}) async-start(), calls=%async_computation | async-start | bytes 3538944 | tf_op jit(solution)/shard_map/psum | solution.py:145
  7.2 11.1 %collective-permute-start = (bf16[2,16,16,128]{3,2,1,0:T(8,128)(2,1)}, bf16[2,16,16,128]{3,2,1,0:T(8,128)(2,1)S(1)}, u32[]{:S(2)}, u32[]{:S(2)}) collective-permute-start(bf16[2,16,16,128]{3,2,1,0:T(8,128)(2,1)} %bitcast.196), channel_id=1, source_target_pairs={{1,0},{3,2},{5,4},{7,6},{9,8},{11,10},{13,12},{15,14},{17,16},{19,... | collective-permute-start | bytes 393224 | tf_op jit(solution)/shard_map/ppermute | solution.py:13
  8.5 2.2 %copy-start.2 = (bf16[1,2,16,16,128]{4,3,2,1,0:T(8,128)(2,1)S(1)}, bf16[1,2,16,16,128]{4,3,2,1,0:T(8,128)(2,1)}, u32[]{:S(2)}) copy-start(bf16[1,2,16,16,128]{4,3,2,1,0:T(8,128)(2,1)} %param.9) | copy-start | bytes 393220
  8.5 7.3 %copy-start = (bf16[1,2,16,16,128]{4,3,2,1,0:T(8,128)(2,1)S(1)}, bf16[1,2,16,16,128]{4,3,2,1,0:T(8,128)(2,1)}, u32[]{:S(2)}) copy-start(bf16[1,2,16,16,128]{4,3,2,1,0:T(8,128)(2,1)} %param.10) | copy-start | bytes 393220
  21.0 0.9 copy-start.3
  21.0 0.9 copy-start.4
  22.1 2.3 %collective-permute-start.1 = (bf16[2,16,16,128]{3,2,1,0:T(8,128)(2,1)S(1)}, bf16[2,16,16,128]{3,2,1,0:T(8,128)(2,1)S(1)}, u32[]{:S(2)}, u32[]{:S(2)}) collective-permute-start(bf16[2,16,16,128]{3,2,1,0:T(8,128)(2,1)S(1)} %get-tuple-element.132), channel_id=1, source_target_pairs={{0,1},{2,3},{4,5},{6,7},{8,9},{10,11},{12,13},{14,15},{16,17},{18,... | collective-permute-start | bytes 393224 | tf_op jit(solution)/shard_map/ppermute | solution.py:13
  28.4 1.2 copy-start.1
  29.7 152.0 %all-reduce.12.cloned.1.call-start = ((), (), s32[]{:S(2)}) async-start(), calls=%async_computation.1 | async-start | bytes 3538944 | tf_op jit(solution)/shard_map/psum | solution.py:144
Sparse Core Ops, SparseCore 0:
  29.8 23.4 all-reduce.9
  58.8 122.8 all-reduce.11
